TPU v7x, 512 devices: a whole 4x8x8 slice. The times are simulated.
512 devices in a mesh: seq: 64 (over z, x, y_hi), ch: 8 (over y_lo, core).
Axes of the slice: x: 4, y: 8 (y_hi: 2, y_lo: 4; y = y_hi * 4 + y_lo), z: 8, core: 2. Of those that a mesh axis runs over, the one named last changes fastest.
Arguments:
- queries: bfloat16 [4096, 8192], P('ch', 'seq'), may hold values from -6 to 6
- key_feat: bfloat16 [4096, 8192], P('ch', 'seq'), may hold values from -6 to 6
- value_feat: bfloat16 [4096, 8192], P('ch', 'seq'), may hold values from -6 to 6
- out_grad: bfloat16 [4096, 8192], P('ch', 'seq'), may hold values from -6 to 6
- out_weight: bfloat16 [4096, 4096], P('ch', 'seq'), may hold values from -0.09375 to 0.09375
- long_filter: bfloat16 [4096, 8192], P('ch', 'seq'), may hold values from -0.125 to 0.125
- short_filter: bfloat16 [256, 128], P('ch'), may hold values from -0.5 to 0.5
Outputs:
- d_key: bfloat16 [4096, 8192], P('ch', 'seq')
- d_value: bfloat16 [4096, 8192], P('ch', 'seq')
- d_filter: float32 [256, 128], P('ch')
All inputs are finite; a program needn't handle non-finite values.
Results may differ from a plain program's by a relative error of at most 0.0064.
Values may be sent and summed in bfloat16 or wider, within the bound.
No kernel may reach another device: no remote copies, remote signals or barrier semaphores. Data moves between devices by JAX's collectives and lax.ppermute only.
A program may use at most 64 MiB of HBM per device.

v0:
```python
import math
import jax
import jax.numpy as jnp
from jax import lax
from jax.sharding import PartitionSpec as P

highest = lax.Precision.HIGHEST


def from_behind(value, axis, steps):
    count = lax.axis_size(axis)
    first, last = (max(0, -steps), min(count, count - steps))
    return lax.ppermute(value, axis, [(source, source + steps) for source in range(first, last)])


def angle_table(first, second, modulus):
    left = lax.broadcasted_iota(jnp.int32, (first, second), 0)
    right = lax.broadcasted_iota(jnp.int32, (first, second), 1)
    phase = (left * right % modulus).astype(jnp.float32) * (2.0 * math.pi / modulus)
    return (jnp.cos(phase), jnp.sin(phase))


def contract(form, first, second):
    return jnp.einsum(form, first, second, precision=highest)


def spectral(pair):
    grads, filters = pair
    items = grads.shape[1]
    seq_len = grads.shape[2]
    inner = 128
    half = seq_len // inner
    outer = 2 * half
    total_len = outer * inner
    cos_p, sin_p = angle_table(outer, half, outer)
    cos_t, sin_t = angle_table(outer, inner, total_len)
    cos_q, sin_q = angle_table(inner, inner, inner)

    def forward(signal):
        series = signal.astype(jnp.float32).reshape(items, half, inner)
        first_re = contract("kn,cnq->ckq", cos_p, series)
        first_im = -contract("kn,cnq->ckq", sin_p, series)
        turned_re = first_re * cos_t + first_im * sin_t
        turned_im = first_im * cos_t - first_re * sin_t
        spec_re = contract("ckq,qm->ckm", turned_re, cos_q) + contract(
            "ckq,qm->ckm", turned_im, sin_q
        )
        spec_im = contract("ckq,qm->ckm", turned_im, cos_q) - contract(
            "ckq,qm->ckm", turned_re, sin_q
        )
        return (spec_re, spec_im)

    grad_re, grad_im = forward(grads[0])
    filt_re, filt_im = forward(filters[0])
    prod_re = filt_re * grad_re + filt_im * grad_im
    prod_im = filt_re * grad_im - filt_im * grad_re
    back_re = contract("ckq,qm->ckm", prod_re, cos_q) - contract("ckq,qm->ckm", prod_im, sin_q)
    back_im = contract("ckq,qm->ckm", prod_im, cos_q) + contract("ckq,qm->ckm", prod_re, sin_q)
    twist_re = back_re * cos_t - back_im * sin_t
    twist_im = back_im * cos_t + back_re * sin_t
    result = contract("kn,ckq->cnq", cos_p, twist_re) - contract("kn,ckq->cnq", sin_p, twist_im)
    return (result / total_len).reshape(1, items, seq_len).astype(jnp.bfloat16)


def windows(extended, group_count, per_group, block_count, tap_count):
    parts = extended.reshape(group_count, per_group, block_count + 1, tap_count)
    return jnp.concatenate([parts[:, :, :-1], parts[:, :, 1:]], axis=3)


def local(queries, key_feat, value_feat, out_grad, out_weight, long_filter, short_filter):
    seq_devices = lax.axis_size("seq")
    channels, row_count = out_grad.shape
    group_count, tap_count = short_filter.shape
    per_group = channels // group_count
    block_count = row_count // tap_count
    per_device = channels // seq_devices
    whole = lax.all_gather(out_grad, "ch", axis=0, tiled=True)
    d_z = jnp.dot(
        lax.all_gather(out_weight, "seq", axis=1, tiled=True),
        whole,
        preferred_element_type=jnp.float32,
    )
    d_c = (d_z * queries.astype(jnp.float32)).astype(jnp.bfloat16)
    packed = (
        d_c.reshape(seq_devices, per_device, row_count),
        long_filter.reshape(seq_devices, per_device, row_count),
    )
    d_w = spectral(
        (
            lax.all_to_all(packed[0], "seq", split_axis=0, concat_axis=2, tiled=True),
            lax.all_to_all(packed[1], "seq", split_axis=0, concat_axis=2, tiled=True),
        )
    )
    prev_rows = from_behind(value_feat, "seq", 1)
    ext_values = jnp.concatenate([prev_rows, value_feat], axis=1)
    value_win = windows(ext_values, group_count, per_group, block_count, tap_count)
    padded_filter = jnp.pad(short_filter, ((0, 0), (0, tap_count + 1)))
    toeplitz = jnp.tile(padded_filter, (1, tap_count))[:, : 2 * tap_count * tap_count]
    toeplitz = toeplitz.reshape(group_count, tap_count, 2 * tap_count)
    reversed_out = jnp.einsum(
        "gtw,gcbw->gcbt", toeplitz, value_win[..., ::-1], preferred_element_type=jnp.float32
    )
    filtered = reversed_out[..., ::-1].reshape(channels, row_count)
    back = lax.all_to_all(d_w, "seq", split_axis=2, concat_axis=0, tiled=True)
    d_w_local = back.reshape(channels, row_count)
    d_vf = (d_w_local.astype(jnp.float32) * key_feat.astype(jnp.float32)).astype(jnp.bfloat16)
    ahead = from_behind(d_vf, "seq", -1)
    ext_grads = jnp.concatenate([d_vf, ahead], axis=1)
    d_key = (d_w_local.astype(jnp.float32) * filtered).astype(jnp.bfloat16)
    grad_win = windows(ext_grads, group_count, per_group, block_count, tap_count)
    d_value = jnp.einsum("gtw,gcbw->gcbt", toeplitz, grad_win, preferred_element_type=jnp.float32)
    d_value = d_value.reshape(channels, row_count).astype(jnp.bfloat16)
    grads_blocked = d_vf.reshape(group_count, per_group, block_count, tap_count)
    corr = jnp.einsum(
        "gcbt,gcbw->gtw", grads_blocked, value_win, preferred_element_type=jnp.float32
    )
    flat = corr.reshape(group_count, 2 * tap_count * tap_count)
    flat = jnp.pad(flat, ((0, 0), (0, tap_count)))
    skewed = flat.reshape(group_count, tap_count, 2 * tap_count + 1)
    column_sums = jnp.sum(skewed, axis=1)
    local_part = column_sums[:, 1 : tap_count + 1][:, ::-1]
    summed = lax.psum(local_part, "seq")
    scale_factor = 1.0 / math.sqrt(row_count * seq_devices * per_group)
    return (d_key, d_value, summed * scale_factor)


def solution(mesh):
    placed = (
        P("ch", "seq"),
        P("ch", "seq"),
        P("ch", "seq"),
        P("ch", "seq"),
        P("ch", "seq"),
        P("ch", "seq"),
        P("ch", None),
    )
    return jax.shard_map(
        local,
        mesh=mesh,
        in_specs=placed,
        out_specs=(P("ch", "seq"), P("ch", "seq"), P("ch", None)),
        check_vma=False,
    )
```

profile of v0, /device:TPU:16, one launch (start us, length us, event | category | flops | bytes accessed | tf_op | source)
XLA Modules:
  0.0 815.4 jit_solution(5035333514818780619)
XLA Ops:
  7.2 0.7 all-gather.5.cloned.1.call-update
  7.9 0.7 all-gather.3.cloned.1.call-update
  8.6 5.9 collective-permute-start
  14.6 15.8 %all-to-all-start = ((bf16[64,8,128]{2,1,0:T(8,128)(2,1)}), bf16[64,8,128]{2,1,0:T(8,128)(2,1)S(1)}, u32[]{:S(2)}, u32[]{:S(2)}) async-start(bf16[64,8,128]{2,1,0:T(8,128)(2,1)} %bitcast.129), calls=%async_computation | async-start | bytes 262144 | tf_op jit(solution)/shard_map/all_to_all | solution.py:91
  30.9 0.7 pad.8
  31.6 2.0 tile.4
  33.5 6.2 tile.10
  39.7 1.6 slice-done
  42.4 1.0 rev.7
  43.4 3.3 all-to-all-done
  47.2 0.6 fusion.34
  47.8 0.8 fusion.10
  48.6 1.6 convolution_add_fusion.2
  50.2 161.0 %all-gather.3.cloned.1.call-done = bf16[512,4096]{0,1:T(8,128)(2,1)} async-done(((bf16[512,64]{0,1:T(8,128)(2,1)}), bf16[512,4096]{0,1:T(8,128)(2,1)}) %all-gather.3.cloned.1.call-update) | async-done | bytes 4194320 | tf_op jit(solution)/shard_map/all_gather | solution.py:79
  211.2 4.5 fusion.5
  215.7 9.9 %all-to-all-start.1 = ((bf16[64,8,128]{2,1,0:T(8,128)(2,1)}), bf16[64,8,128]{2,1,0:T(8,128)(2,1)S(1)}, u32[]{:S(2)}, u32[]{:S(2)}) async-start(bf16[64,8,128]{2,1,0:T(8,128)(2,1)} %fusion.5), calls=%async_computation.1 | async-start | bytes 262144 | tf_op jit(solution)/shard_map/all_to_all | solution.py:90
  225.7 1.6 fusion.6
  227.3 13.1 %all-to-all-done.1 = bf16[64,8,128]{2,1,0:T(8,128)(2,1)S(1)} async-done(((bf16[64,8,128]{2,1,0:T(8,128)(2,1)}), bf16[64,8,128]{2,1,0:T(8,128)(2,1)S(1)}, u32[]{:S(2)}, u32[]{:S(2)}) %all-to-all-start.1) | async-done | bytes 131104 | tf_op jit(solution)/shard_map/all_to_all | solution.py:90
  241.5 1.2 fusion.41
  242.7 1.2 fusion.40
  243.9 1.2 convolution_subtract_fusion.1
  245.1 1.2 convolution_add_fusion.1
  246.4 0.9 multiply_add_fusion
  247.3 0.9 fusion.52
  248.1 0.9 fusion.54
  249.0 0.9 convolution_add_fusion
  249.9 0.9 convolution_subtract_fusion
  250.7 0.9 fusion.15
  251.6 1.1 fusion.4
  252.8 6.7 copy.55
  260.0 46.6 %reduce = bf16[8192,8]{1,0:T(8,128)(2,1)} reduce(bf16[8192,1,8]{2,1,0:T(2,128)(2,1)} %bitcast.122, bf16[]{:T(256)} %broadcast.142), dimensions={1}, to_apply=%bitcast.104.reduce_sub_computation | reduce | bytes 262146
  306.6 4.3 reshape.131
  310.9 4.6 all-to-all-start.2
  315.5 0.6 fusion.24
  316.3 13.9 %all-to-all-done.2 = bf16[64,2,512]{2,1,0:T(2,128)(2,1)S(1)} async-done(((bf16[64,2,512]{2,1,0:T(2,128)(2,1)}), bf16[64,2,512]{2,1,0:T(2,128)(2,1)S(1)}, u32[]{:S(2)}, u32[]{:S(2)}) %all-to-all-start.2) | async-done | bytes 131104 | tf_op jit(solution)/shard_map/all_to_all | solution.py:104
  330.2 8.7 %reshape.132 = bf16[8192,1,8]{2,1,0:T(2,128)(2,1)} reshape(bf16[64,2,512]{2,1,0:T(2,128)(2,1)S(1)} %all-to-all-done.2) | data formatting | bytes 262144
  338.9 8.5 %bitcast_convert_fusion = f32[1,8,8192]{1,0,2:T(1,128)} fusion(bf16[8192,1,8]{2,1,0:T(2,128)(2,1)} %reshape.132), kind=kLoop, calls=%fused_computation.195 | loop fusion | flops 65536 | bytes 393216 | tf_op jit(solution)/shard_map/convert_element_type | solution.py:109
  347.4 2.8 copy.56
  350.2 0.7 fusion.26
  350.9 1.5 collective-permute-start.1
  352.4 0.7 fusion.21
  353.2 2.4 copy.76
  355.6 2.3 pad.9
  357.9 8.0 reshape.124
  365.9 3.3 reduce_sum.9
  369.4 436.5 %psum.7 = f32[32,128]{1,0:T(8,128)S(1)} all-reduce(f32[32,128]{1,0:T(8,128)S(1)} %rev.8), channel_id=1, replica_groups=mesh['seq'=64,'ch'=8] {'seq'}, use_global_device_ids=true, to_apply=%region_1.2 | all-reduce | flops 4096 | bytes 32768 | tf_op jit(solution)/shard_map/psum | solution.py:122
  805.9 0.6 broadcast_multiply_fusion
  807.0 1.3 convolution_convert_fusion
  (42 shorter events, 4.5 us)
Async XLA Ops:
  7.2 43.0 %all-gather.5.cloned.1.call-start = ((), (), s32[]{:S(2)}) async-start(), calls=%async_computation.4 | async-start | bytes 1179648 | tf_op jit(solution)/shard_map/all_gather | solution.py:77
  7.9 203.3 %all-gather.3.cloned.1.call-start = ((), (), s32[]{:S(2)}) async-start(), calls=%async_computation.3 | async-start | bytes 4259840 | tf_op jit(solution)/shard_map/all_gather | solution.py:79
  8.6 33.2 %collective-permute-start = (bf16[512,128]{1,0:T(8,128)(2,1)}, bf16[512,128]{1,0:T(8,128)(2,1)S(1)}, u32[]{:S(2)}, u32[]{:S(2)}) collective-permute-start(bf16[512,128]{1,0:T(8,128)(2,1)} %param.9), channel_id=1, source_target_pairs={{0,8},{8,16},{16,24},{24,32},{32,40},{40,48},{48,56},{56,64},{64,7... | collective-permute-start | bytes 393224 | tf_op jit(solution)/shard_map/ppermute | solution.py:13
  14.6 32.1 %all-to-all-start = ((bf16[64,8,128]{2,1,0:T(8,128)(2,1)}), bf16[64,8,128]{2,1,0:T(8,128)(2,1)S(1)}, u32[]{:S(2)}, u32[]{:S(2)}) async-start(bf16[64,8,128]{2,1,0:T(8,128)(2,1)} %bitcast.129), calls=%async_computation | async-start | bytes 262144 | tf_op jit(solution)/shard_map/all_to_all | solution.py:91
  39.7 1.6 slice-start
  39.7 2.1 copy-start.6
  42.4 1.0 copy-start.2
  215.7 24.7 %all-to-all-start.1 = ((bf16[64,8,128]{2,1,0:T(8,128)(2,1)}), bf16[64,8,128]{2,1,0:T(8,128)(2,1)S(1)}, u32[]{:S(2)}, u32[]{:S(2)}) async-start(bf16[64,8,128]{2,1,0:T(8,128)(2,1)} %fusion.5), calls=%async_computation.1 | async-start | bytes 262144 | tf_op jit(solution)/shard_map/all_to_all | solution.py:90
  240.9 5.4 copy-start
  240.9 5.4 copy-start.1
  260.0 55.6 %copy-start.4 = (bf16[32,16,1,256]{3,1,0,2:T(8,128)(2,1)S(1)}, bf16[32,16,1,256]{3,1,0,2:T(8,128)(2,1)}, u32[]{:S(2)}) copy-start(bf16[32,16,1,256]{3,1,0,2:T(8,128)(2,1)} %rev.7) | copy-start | bytes 786436
  310.9 19.3 %all-to-all-start.2 = ((bf16[64,2,512]{2,1,0:T(2,128)(2,1)}), bf16[64,2,512]{2,1,0:T(2,128)(2,1)S(1)}, u32[]{:S(2)}, u32[]{:S(2)}) async-start(bf16[64,2,512]{2,1,0:T(2,128)(2,1)} %reshape.131), calls=%async_computation.2 | async-start | bytes 262144 | tf_op jit(solution)/shard_map/all_to_all | solution.py:104
  347.4 2.8 copy-start.5
  347.4 5.1 copy-start.3
  350.9 455.6 %collective-permute-start.1 = (bf16[512,128]{1,0:T(8,128)(2,1)S(1)}, bf16[512,128]{1,0:T(8,128)(2,1)S(1)}, u32[]{:S(2)}, u32[]{:S(2)}) collective-permute-start(bf16[512,128]{1,0:T(8,128)(2,1)S(1)} %get-tuple-element.7), channel_id=1, source_target_pairs={{8,0},{16,8},{24,16},{32,24},{40,32},{48,40},{56,48},{64,56},{72,6... | collective-permute-start | bytes 393224 | tf_op jit(solution)/shard_map/ppermute | solution.py:13
Sparse Core Ops, SparseCore 0:
  10.0 38.5 all-gather.4
  53.0 158.1 all-gather.2
where the time goes:
time: 823 us; the launch traced here: 815 us
  blocking collectives  436 us (53%)
  waiting for transfers between devices  193 us (23%)
  other arithmetic  60 us (7%)
  local copies, waits for them, and re-layouts  49.3 us (6%)
  starting transfers between devices  37.8 us (5%)
  matrix products  24.5 us (3%)
  between operations  14.6 us (2%)
    psum x1, blocking collectives, local(): summed = lax.psum(local_part, 'seq')  436 us
    all_gather x1, waiting for transfers between devices, local(): lax.all_gather(out_weight, 'seq', axis=1, tiled=True)  161 us
    unnamed x1, other arithmetic  46.6 us
    dot_general x18, matrix products, contract(): return jnp.einsum(form, first, second, precision=highest)  17.3 us
    unnamed x22, local copies, waits for them, and re-layouts  16.5 us
  transfers between devices with their start and end apart: 7, of which 4 were waited for; matrix products, arithmetic and copies ran while one was open for 4% of the time, Pallas kernels for 0%

commit v1 on v0

--- a/solution.py
+++ b/solution.py
@@ -119,7 +119,7 @@
     skewed = flat.reshape(group_count, tap_count, 2 * tap_count + 1)
     column_sums = jnp.sum(skewed, axis=1)
     local_part = column_sums[:, 1 : tap_count + 1][:, ::-1]
-    summed = lax.psum(local_part, "seq")
+    summed = jnp.sum(lax.all_gather(local_part, "seq"), axis=0)
     scale_factor = 1.0 / math.sqrt(row_count * seq_devices * per_group)
     return (d_key, d_value, summed * scale_factor)
 

time: 823 us -> 505 us (0.61)
  the two profiles are of different devices: /device:TPU:16 before, /device:TPU:2 now
where the time goes in v1:
time: 505 us; the launch traced here: 497 us
  waiting for transfers between devices  307 us (61%)
  other arithmetic  61.4 us (12%)
  local copies, waits for them, and re-layouts  50.1 us (10%)
  starting transfers between devices  39.9 us (8%)
  matrix products  24.5 us (5%)
  between operations  14.3 us (3%)
    all_gather x1, waiting for transfers between devices, local(): lax.all_gather(out_weight, 'seq', axis=1, tiled=True)  158 us
    all_gather x1, waiting for transfers between devices, local(): summed = jnp.sum(lax.all_gather(local_part, 'seq'), axis=0)  109 us
    unnamed x1, other arithmetic  46.6 us
    dot_general x18, matrix products, contract(): return jnp.einsum(form, first, second, precision=highest)  17.3 us
    unnamed x22, local copies, waits for them, and re-layouts  16.7 us
    all_to_all x1, starting transfers between devices, local(): lax.all_to_all(packed[1], 'seq', split_axis=0, concat_axis=2, tiled=True)  14.1 us
    all_to_all x1, waiting for transfers between devices, local(): back = lax.all_to_all(d_w, 'seq', split_axis=2, concat_axis=0, tiled=True)  12.9 us
    ppermute x2, starting transfers between devices, from_behind(): lax.ppermute(value, axis, [(source, source + steps) for source in range(f...  11.8 us
  transfers between devices with their start and end apart: 8, of which 7 were waited for; matrix products, arithmetic and copies ran while one was open for 4% of the time, Pallas kernels for 0%

profile of v1, /device:TPU:2, one launch (start us, length us, event | category | flops | bytes accessed | tf_op | source)
XLA Modules:
  0.0 497.4 jit_solution(875422276125203666)
XLA Ops:
  7.2 0.7 all-gather.7.cloned.1.call-update
  7.9 0.7 all-gather.5.cloned.1.call-update
  8.6 7.7 %collective-permute-start = (bf16[512,128]{1,0:T(8,128)(2,1)}, bf16[512,128]{1,0:T(8,128)(2,1)S(1)}, u32[]{:S(2)}, u32[]{:S(2)}) collective-permute-start(bf16[512,128]{1,0:T(8,128)(2,1)} %param.9), channel_id=1, source_target_pairs={{0,8},{8,16},{16,24},{24,32},{32,40},{40,48},{48,56},{56,64},{64,7... | collective-permute-start | bytes 393224 | tf_op jit(solution)/shard_map/ppermute | solution.py:13
  16.4 14.1 %all-to-all-start = ((bf16[64,8,128]{2,1,0:T(8,128)(2,1)}), bf16[64,8,128]{2,1,0:T(8,128)(2,1)S(1)}, u32[]{:S(2)}, u32[]{:S(2)}) async-start(bf16[64,8,128]{2,1,0:T(8,128)(2,1)} %bitcast.131), calls=%async_computation | async-start | bytes 262144 | tf_op jit(solution)/shard_map/all_to_all | solution.py:91
  30.9 0.7 pad.8
  31.6 2.0 tile.4
  33.6 6.2 %tile.10 = bf16[32,32896]{1,0:T(8,128)(2,1)} reshape(bf16[32,128,257]{2,1,0:T(8,128)(2,1)} %tile.4) | data formatting | bytes 4210688 | tf_op jit(solution)/shard_map/tile | solution.py:98
  39.8 1.6 slice-done
  42.5 1.0 rev.7
  43.5 2.7 all-to-all-done
  47.3 0.8 fusion.10
  48.1 1.6 convolution_add_fusion.2
  49.7 5.2 %all-gather.7.cloned.1.call-done = bf16[4096,128]{1,0:T(8,128)(2,1)} async-done(((bf16[512,128]{1,0:T(8,128)(2,1)}), bf16[4096,128]{1,0:T(8,128)(2,1)}) %all-gather.7.cloned.1.call-update) | async-done | bytes 1048592 | tf_op jit(solution)/shard_map/all_gather | solution.py:77
  54.9 158.1 %all-gather.5.cloned.1.call-done = bf16[512,4096]{0,1:T(8,128)(2,1)} async-done(((bf16[512,64]{0,1:T(8,128)(2,1)}), bf16[512,4096]{0,1:T(8,128)(2,1)}) %all-gather.5.cloned.1.call-update) | async-done | bytes 4194320 | tf_op jit(solution)/shard_map/all_gather | solution.py:79
  213.0 4.5 fusion.5
  217.5 8.4 %all-to-all-start.1 = ((bf16[64,8,128]{2,1,0:T(8,128)(2,1)}), bf16[64,8,128]{2,1,0:T(8,128)(2,1)S(1)}, u32[]{:S(2)}, u32[]{:S(2)}) async-start(bf16[64,8,128]{2,1,0:T(8,128)(2,1)} %fusion.5), calls=%async_computation.1 | async-start | bytes 262144 | tf_op jit(solution)/shard_map/all_to_all | solution.py:90
  225.8 1.6 fusion.6
  227.5 11.6 %all-to-all-done.1 = bf16[64,8,128]{2,1,0:T(8,128)(2,1)S(1)} async-done(((bf16[64,8,128]{2,1,0:T(8,128)(2,1)}), bf16[64,8,128]{2,1,0:T(8,128)(2,1)S(1)}, u32[]{:S(2)}, u32[]{:S(2)}) %all-to-all-start.1) | async-done | bytes 131104 | tf_op jit(solution)/shard_map/all_to_all | solution.py:90
  240.1 1.2 fusion.41
  241.3 1.2 fusion.40
  242.5 1.2 convolution_subtract_fusion.1
  243.8 1.2 convolution_add_fusion.1
  245.0 0.9 multiply_add_fusion
  245.9 0.9 fusion.52
  246.8 0.9 fusion.54
  247.6 0.9 convolution_add_fusion
  248.5 0.9 convolution_subtract_fusion
  249.4 0.9 fusion.15
  250.3 1.1 fusion.4
  251.4 6.8 %copy.75 = bf16[1,8,8192]{1,0,2:T(2,128)(2,1)} copy(bf16[1,8,8192]{2,1,0:T(8,128)(2,1)S(1)} %convert_element_type.134) | data formatting | bytes 262144 | tf_op jit(solution)/shard_map/convert_element_type | solution.py:62
  258.6 46.6 %reduce = bf16[8192,8]{1,0:T(8,128)(2,1)} reduce(bf16[8192,1,8]{2,1,0:T(2,128)(2,1)} %bitcast.123, bf16[]{:T(256)} %broadcast.142), dimensions={1}, to_apply=%bitcast.105.reduce_sub_computation | reduce | bytes 262146
  305.2 4.3 reshape.132
  309.6 5.5 %all-to-all-start.2 = ((bf16[64,2,512]{2,1,0:T(2,128)(2,1)}), bf16[64,2,512]{2,1,0:T(2,128)(2,1)S(1)}, u32[]{:S(2)}, u32[]{:S(2)}) async-start(bf16[64,2,512]{2,1,0:T(2,128)(2,1)} %reshape.132), calls=%async_computation.2 | async-start | bytes 262144 | tf_op jit(solution)/shard_map/all_to_all | solution.py:104
  315.9 12.9 %all-to-all-done.2 = bf16[64,2,512]{2,1,0:T(2,128)(2,1)S(1)} async-done(((bf16[64,2,512]{2,1,0:T(2,128)(2,1)}), bf16[64,2,512]{2,1,0:T(2,128)(2,1)S(1)}, u32[]{:S(2)}, u32[]{:S(2)}) %all-to-all-start.2) | async-done | bytes 131104 | tf_op jit(solution)/shard_map/all_to_all | solution.py:104
  328.8 8.9 %reshape.133 = bf16[8192,1,8]{2,1,0:T(2,128)(2,1)} reshape(bf16[64,2,512]{2,1,0:T(2,128)(2,1)S(1)} %all-to-all-done.2) | data formatting | bytes 262144
  337.7 8.5 %bitcast_convert_fusion = f32[1,8,8192]{1,0,2:T(1,128)} fusion(bf16[8192,1,8]{2,1,0:T(2,128)(2,1)} %reshape.133), kind=kLoop, calls=%fused_computation.195 | loop fusion | flops 65536 | bytes 393216 | tf_op jit(solution)/shard_map/convert_element_type | solution.py:109
  346.2 2.8 copy.76
  349.1 0.7 fusion.26
  349.8 0.7 fusion.21
  350.5 2.4 copy.96
  353.0 2.3 pad.9
  355.3 8.0 %reshape.124 = f32[32,128,257]{2,1,0:T(8,128)} reshape(f32[32,32896]{1,0:T(8,128)} %pad.9) | data formatting | bytes 8421376 | tf_op jit(solution)/shard_map/reshape | solution.py:119
  363.3 3.3 reduce_sum.18
  367.4 4.1 collective-permute-start.1
  371.5 6.8 %collective-permute-done.1 = bf16[512,128]{1,0:T(8,128)(2,1)S(1)} collective-permute-done((bf16[512,128]{1,0:T(8,128)(2,1)S(1)}, bf16[512,128]{1,0:T(8,128)(2,1)S(1)}, u32[]{:S(2)}, u32[]{:S(2)}) %collective-permute-start.1) | collective-permute-done | bytes 131104 | tf_op jit(solution)/shard_map/ppermute | solution.py:13
  378.8 1.3 convolution_convert_fusion
  380.1 108.6 %all-gather.9.cloned.1.call-done = f32[2048,128]{1,0:T(8,128)} async-done(((f32[32,128]{1,0:T(8,128)}), f32[2048,128]{1,0:T(8,128)}) %all-gather.9.cloned.1.call-update) | async-done | bytes 1048592 | tf_op jit(solution)/shard_map/all_gather | solution.py:122
  488.7 1.3 reduce_sum.19
  (45 shorter events, 7.0 us)
Async XLA Ops:
  7.2 47.7 %all-gather.7.cloned.1.call-start = ((), (), s32[]{:S(2)}) async-start(), calls=%async_computation.4 | async-start | bytes 1179648 | tf_op jit(solution)/shard_map/all_gather | solution.py:77
  7.9 205.1 %all-gather.5.cloned.1.call-start = ((), (), s32[]{:S(2)}) async-start(), calls=%async_computation.3 | async-start | bytes 4259840 | tf_op jit(solution)/shard_map/all_gather | solution.py:79
  8.6 33.3 %collective-permute-start = (bf16[512,128]{1,0:T(8,128)(2,1)}, bf16[512,128]{1,0:T(8,128)(2,1)S(1)}, u32[]{:S(2)}, u32[]{:S(2)}) collective-permute-start(bf16[512,128]{1,0:T(8,128)(2,1)} %param.9), channel_id=1, source_target_pairs={{0,8},{8,16},{16,24},{24,32},{32,40},{40,48},{48,56},{56,64},{64,7... | collective-permute-start | bytes 393224 | tf_op jit(solution)/shard_map/ppermute | solution.py:13
  16.4 29.8 %all-to-all-start = ((bf16[64,8,128]{2,1,0:T(8,128)(2,1)}), bf16[64,8,128]{2,1,0:T(8,128)(2,1)S(1)}, u32[]{:S(2)}, u32[]{:S(2)}) async-start(bf16[64,8,128]{2,1,0:T(8,128)(2,1)} %bitcast.131), calls=%async_computation | async-start | bytes 262144 | tf_op jit(solution)/shard_map/all_to_all | solution.py:91
  39.8 1.6 slice-start
  39.8 2.1 copy-start.6
  42.5 1.0 copy-start.2
  217.5 21.6 %all-to-all-start.1 = ((bf16[64,8,128]{2,1,0:T(8,128)(2,1)}), bf16[64,8,128]{2,1,0:T(8,128)(2,1)S(1)}, u32[]{:S(2)}, u32[]{:S(2)}) async-start(bf16[64,8,128]{2,1,0:T(8,128)(2,1)} %fusion.5), calls=%async_computation.1 | async-start | bytes 262144 | tf_op jit(solution)/shard_map/all_to_all | solution.py:90
  239.6 5.4 %copy-start = (f32[8,128,128]{2,1,0:T(8,128)S(1)}, f32[8,128,128]{2,1,0:T(8,128)}, u32[]{:S(2)}) copy-start(f32[8,128,128]{2,1,0:T(8,128)} %convolution_add_fusion.2) | copy-start | bytes 1572868
  239.6 5.4 %copy-start.1 = (f32[8,128,128]{2,1,0:T(8,128)S(1)}, f32[8,128,128]{2,1,0:T(8,128)}, u32[]{:S(2)}) copy-start(f32[8,128,128]{2,1,0:T(8,128)} %fusion.6) | copy-start | bytes 1572868
  258.6 56.5 %copy-start.4 = (bf16[32,16,1,256]{3,1,0,2:T(8,128)(2,1)S(1)}, bf16[32,16,1,256]{3,1,0,2:T(8,128)(2,1)}, u32[]{:S(2)}) copy-start(bf16[32,16,1,256]{3,1,0,2:T(8,128)(2,1)} %rev.7) | copy-start | bytes 786436
  309.6 19.3 %all-to-all-start.2 = ((bf16[64,2,512]{2,1,0:T(2,128)(2,1)}), bf16[64,2,512]{2,1,0:T(2,128)(2,1)S(1)}, u32[]{:S(2)}, u32[]{:S(2)}) async-start(bf16[64,2,512]{2,1,0:T(2,128)(2,1)} %reshape.132), calls=%async_computation.2 | async-start | bytes 262144 | tf_op jit(solution)/shard_map/all_to_all | solution.py:104
  315.1 173.7 %all-gather.9.cloned.1.call-start = ((), (), s32[]{:S(2)}) async-start(), calls=%async_computation.5 | async-start | bytes 1064960 | tf_op jit(solution)/shard_map/all_gather | solution.py:122
  346.2 2.8 copy-start.5
  346.2 3.6 copy-start.3
  367.4 10.8 %collective-permute-start.1 = (bf16[512,128]{1,0:T(8,128)(2,1)S(1)}, bf16[512,128]{1,0:T(8,128)(2,1)S(1)}, u32[]{:S(2)}, u32[]{:S(2)}) collective-permute-start(bf16[512,128]{1,0:T(8,128)(2,1)S(1)} %get-tuple-element.7), channel_id=1, source_target_pairs={{8,0},{16,8},{24,16},{32,24},{40,32},{48,40},{56,48},{64,56},{72,6... | collective-permute-start | bytes 393224 | tf_op jit(solution)/shard_map/ppermute | solution.py:13
Sparse Core Ops, SparseCore 0:
  10.0 44.7 all-gather.6
  59.2 153.7 all-gather.4
  367.5 121.1 all-gather.8
